TPU v7x, 512 devices: a whole 4x8x8 slice. The times are simulated.
512 devices in a mesh: grp: 8 (over x, z_lo), req: 64 (over y, z_hi, core).
Axes of the slice: x: 4, y: 8, z: 8 (z_hi: 4, z_lo: 2; z = z_hi * 2 + z_lo), core: 2. Of those that a mesh axis runs over, the one named last changes fastest.
Arguments:
- queries: bfloat16 [8, 8192, 1024], P('grp', 'req')
- suffix_kv: bfloat16 [8, 2, 8192, 1024], P('grp', None, 'req')
- prefix_kv: bfloat16 [8, 2, 1024, 1024], P('grp', None, 'req'), may hold values from -6 to 6
- lengths: int32 [8, 12], P('grp'), may hold values from 1 to 2048, 8192 in all within a row
Outputs:
- attended: bfloat16 [8, 8192, 1024], P('grp', 'req')
Inputs may be any that keep to these rules, and one draw needn't show every extreme that they name: Each group's 12 lengths sum to 8192, the longest exactly 2048.
All inputs are finite; a program needn't handle non-finite values.
Results may differ from a plain program's by a relative error of at most 0.0075.
Values may be sent and summed in bfloat16 or wider, within the bound.
A program may use at most 64 MiB of HBM per device.

v0:
```python
import jax
import jax.numpy as jnp
from jax import lax
from jax.sharding import PartitionSpec as P

HEADS = 16
HEAD = 64
WIN = 1024


def from_behind(block, axis, distance):
    devices = range(lax.axis_size(axis))
    route = [(i - distance, i) for i in devices if i - distance in devices]
    return lax.ppermute(block, axis, route)


def locate(positions, starts, ends):
    inside = (positions[:, None] >= starts[None, :]) & (positions[:, None] < ends[None, :])
    numbers = jnp.arange(1, starts.shape[0] + 1, dtype=jnp.int32)
    request = jnp.sum(jnp.where(inside, numbers[None, :], 0), axis=1) - 1
    offset = positions - jnp.sum(jnp.where(inside, starts[None, :], 0), axis=1)
    return (request, offset)


def absorb(carry, query, keys, vals, mask):
    running_max, running_total, running_acc = carry
    score = jnp.einsum("qhd,khd->hqk", query, keys, preferred_element_type=jnp.float32) * 0.125
    score = jnp.where(mask[None], score, -1e30)
    new_max = jnp.maximum(running_max, jnp.max(score, axis=-1))
    factor = jnp.exp(running_max - new_max)
    weight = jnp.where(mask[None], jnp.exp(score - new_max[..., None]), 0.0)
    new_total = running_total * factor + jnp.sum(weight, axis=-1)
    rounded = weight.astype(jnp.bfloat16)
    added = jnp.einsum("hqk,khd->hqd", rounded, vals, preferred_element_type=jnp.float32)
    return (new_max, new_total, running_acc * factor[..., None] + added)


def on_device(queries, suffix_kv, prefix_kv, lengths):
    tok_rows = queries.shape[1]
    width = queries.shape[2]
    req_count = lax.axis_size("req")
    position = lax.axis_index("req")
    lens = lengths[0]
    ends = jnp.cumsum(lens)
    starts = ends - lens
    query_index = position * tok_rows + jnp.arange(tok_rows, dtype=jnp.int32)
    query_req, query_off = locate(query_index, starts, ends)
    query = queries[0].reshape(tok_rows, HEADS, HEAD)

    def near_block(carry, block, distance):
        key_index = (position - distance) * tok_rows + jnp.arange(tok_rows, dtype=jnp.int32)
        key_req, key_off = locate(key_index, starts, ends)
        mask = (key_req[None, :] == query_req[:, None]) & (key_off[None, :] <= query_off[:, None])
        mask = mask & (query_off[:, None] - key_off[None, :] < WIN) & (key_index[None, :] >= 0)
        keys = block[0, 0].reshape(tok_rows, HEADS, HEAD)
        vals = block[0, 1].reshape(tok_rows, HEADS, HEAD)
        return absorb(carry, query, keys, vals, mask)

    carry = (
        jnp.full((HEADS, tok_rows), -1e30, jnp.float32),
        jnp.zeros((HEADS, tok_rows), jnp.float32),
        jnp.zeros((HEADS, tok_rows, HEAD), jnp.float32),
    )
    carry = near_block(carry, suffix_kv, 0)
    reach = min((WIN + tok_rows - 1) // tok_rows, req_count - 1)
    current = suffix_kv
    for distance in range(1, reach + 1):
        current = from_behind(current, "req", 1)
        carry = near_block(carry, current, distance)
    piece = lax.all_gather(prefix_kv, "req", axis=2, tiled=True)
    count = piece.shape[2]
    cached = jnp.arange(count, dtype=jnp.int32)
    mask = cached[None, :] > query_off[:, None]
    keys = piece[0, 0].reshape(count, HEADS, HEAD)
    vals = piece[0, 1].reshape(count, HEADS, HEAD)
    carry = absorb(carry, query, keys, vals, mask)
    final_max, final_total, final_acc = carry
    attended = final_acc / final_total[..., None]
    attended = jnp.transpose(attended, (1, 0, 2)).reshape(tok_rows, width).astype(jnp.bfloat16)
    return attended[None]


def solution(mesh):
    in_specs = (
        P("grp", "req", None),
        P("grp", None, "req", None),
        P("grp", None, "req", None),
        P("grp", None),
    )
    out_specs = P("grp", "req", None)
    return jax.shard_map(
        on_device, mesh=mesh, in_specs=in_specs, out_specs=out_specs, check_vma=False
    )
```

profile of v0, /device:TPU:36, one launch (start us, length us, event | category | flops | bytes accessed | tf_op | source)
XLA Modules:
  0.0 212.9 jit_solution(11425991582510790491)
XLA Ops:
  6.5 0.7 all-gather.2.cloned.1.call-update
  7.3 1.9 collective-permute-start
  9.4 0.8 reduce-window.4
  10.2 0.7 fusion.124
  11.1 19.1 %collective-permute-done = bf16[1,2,128,1024]{3,2,1,0:T(8,128)(2,1)S(1)} collective-permute-done((bf16[1,2,128,1024]{3,2,1,0:T(8,128)(2,1)}, bf16[1,2,128,1024]{3,2,1,0:T(8,128)(2,1)S(1)}, u32[]{:S(2)}, u32[]{:S(2)}) %collective-permute-start) | collective-permute-done | bytes 524320 | tf_op jit(solution)/shard_map/ppermute | solution.py:14
  30.2 1.9 collective-permute-start.1
  32.1 1.1 fusion.94
  33.3 1.1 fusion.159
  34.4 16.1 %collective-permute-done.1 = bf16[1,2,128,1024]{3,2,1,0:T(8,128)(2,1)S(1)} collective-permute-done((bf16[1,2,128,1024]{3,2,1,0:T(8,128)(2,1)S(1)}, bf16[1,2,128,1024]{3,2,1,0:T(8,128)(2,1)S(1)}, u32[]{:S(2)}, u32[]{:S(2)}) %collective-permute-start.1) | collective-permute-done | bytes 524320 | tf_op jit(solution)/shard_map/ppermute | solution.py:14
  50.5 1.9 collective-permute-start.2
  52.4 0.8 fusion.100
  53.2 1.1 copy.76
  54.5 0.9 copy.78
  55.5 1.0 fusion.168
  56.5 13.7 %collective-permute-done.2 = bf16[1,2,128,1024]{3,2,1,0:T(8,128)(2,1)} collective-permute-done((bf16[1,2,128,1024]{3,2,1,0:T(8,128)(2,1)S(1)}, bf16[1,2,128,1024]{3,2,1,0:T(8,128)(2,1)}, u32[]{:S(2)}, u32[]{:S(2)}) %collective-permute-start.2) | collective-permute-done | bytes 524320 | tf_op jit(solution)/shard_map/ppermute | solution.py:14
  70.2 1.9 collective-permute-start.3
  72.4 0.9 copy.81
  73.2 1.0 fusion.167
  74.2 1.9 fusion.157
  76.0 0.8 copy.83
  76.9 13.9 %collective-permute-done.3 = bf16[1,2,128,1024]{3,2,1,0:T(8,128)(2,1)} collective-permute-done((bf16[1,2,128,1024]{3,2,1,0:T(8,128)(2,1)}, bf16[1,2,128,1024]{3,2,1,0:T(8,128)(2,1)}, u32[]{:S(2)}, u32[]{:S(2)}) %collective-permute-start.3) | collective-permute-done | bytes 524320 | tf_op jit(solution)/shard_map/ppermute | solution.py:14
  90.8 1.9 collective-permute-start.4
  92.8 1.9 fusion.166
  94.7 1.8 copy.84
  96.5 1.9 fusion.156
  98.4 1.8 copy.86
  100.2 1.8 copy.87
  102.0 3.0 %fusion.165 = (f32[16,128]{1,0:T(8,128)}, f32[16,128,128]{1,2,0:T(8,128)}) fusion(bf16[128,16,64]{0,2,1:T(8,128)(2,1)S(1)} %bitcast.266, bf16[128,16,64]{0,2,1:T(8,128)(2,1)} %bitcast.288, pred[128,128]{0,1:T(8,128)(4,1)} %get-tuple-element.73), kind=kOutput, calls=%fused_computation.275 | convolution fusion | flops 34338816 | bytes 1597440 | tf_op jit(solution)/shard_map/qhd,khd->hqk/dot_general | solution.py:27
  104.9 6.2 %collective-permute-done.4 = bf16[1,2,128,1024]{3,2,1,0:T(8,128)(2,1)} collective-permute-done((bf16[1,2,128,1024]{3,2,1,0:T(8,128)(2,1)}, bf16[1,2,128,1024]{3,2,1,0:T(8,128)(2,1)}, u32[]{:S(2)}, u32[]{:S(2)}) %collective-permute-start.4) | collective-permute-done | bytes 524320 | tf_op jit(solution)/shard_map/ppermute | solution.py:14
  111.1 1.9 collective-permute-start.5
  113.1 1.9 fusion.155
  114.9 1.8 copy.89
  116.7 1.8 copy.90
  118.5 2.9 %fusion.164 = (f32[16,128]{1,0:T(8,128)}, f32[16,128,128]{1,2,0:T(8,128)}) fusion(bf16[128,16,64]{0,2,1:T(8,128)(2,1)S(1)} %bitcast.267, bf16[128,16,64]{0,2,1:T(8,128)(2,1)} %bitcast.289, pred[128,128]{0,1:T(8,128)(4,1)} %get-tuple-element.75), kind=kOutput, calls=%fused_computation.274 | convolution fusion | flops 34338816 | bytes 1597440 | tf_op jit(solution)/shard_map/qhd,khd->hqk/dot_general | solution.py:27
  121.4 1.9 fusion.154
  123.3 1.8 copy.92
  125.1 6.8 %collective-permute-done.5 = bf16[1,2,128,1024]{3,2,1,0:T(8,128)(2,1)} collective-permute-done((bf16[1,2,128,1024]{3,2,1,0:T(8,128)(2,1)}, bf16[1,2,128,1024]{3,2,1,0:T(8,128)(2,1)}, u32[]{:S(2)}, u32[]{:S(2)}) %collective-permute-start.5) | collective-permute-done | bytes 524320 | tf_op jit(solution)/shard_map/ppermute | solution.py:14
  131.9 1.9 collective-permute-start.6
  133.8 2.9 %fusion.163 = (f32[16,128]{1,0:T(8,128)}, f32[16,128,128]{1,2,0:T(8,128)}) fusion(bf16[128,16,64]{0,2,1:T(8,128)(2,1)S(1)} %bitcast.268, bf16[128,16,64]{0,2,1:T(8,128)(2,1)} %bitcast.283, pred[128,128]{0,1:T(8,128)(4,1)} %get-tuple-element.70), kind=kOutput, calls=%fused_computation.273 | convolution fusion | flops 34338816 | bytes 1597440 | tf_op jit(solution)/shard_map/qhd,khd->hqk/dot_general | solution.py:27
  136.7 1.8 copy.93
  138.5 1.9 fusion.153
  140.4 1.8 copy.95
  142.1 2.3 %fusion.162 = (f32[16,128]{1,0:T(8,128)S(1)}, f32[16,128,128]{1,2,0:T(8,128)}) fusion(bf16[128,16,64]{0,2,1:T(8,128)(2,1)S(1)} %bitcast.269, bf16[128,16,64]{0,2,1:T(8,128)(2,1)} %bitcast.291, pred[128,128]{0,1:T(8,128)(4,1)S(1)} %get-tuple-element.74), kind=kOutput, calls=%fused_computation.272 | convolution fusion | flops 34338816 | bytes 1597440 | tf_op jit(solution)/shard_map/qhd,khd->hqk/dot_general | solution.py:27
  144.4 7.2 %collective-permute-done.6 = bf16[1,2,128,1024]{3,2,1,0:T(8,128)(2,1)} collective-permute-done((bf16[1,2,128,1024]{3,2,1,0:T(8,128)(2,1)}, bf16[1,2,128,1024]{3,2,1,0:T(8,128)(2,1)}, u32[]{:S(2)}, u32[]{:S(2)}) %collective-permute-start.6) | collective-permute-done | bytes 524320 | tf_op jit(solution)/shard_map/ppermute | solution.py:14
  151.6 2.1 collective-permute-start.7
  153.7 1.4 bitcast_maximum_fusion.2
  155.1 1.8 copy.96
  156.9 1.8 fusion.152
  158.8 1.8 copy.98
  160.6 1.8 copy.99
  162.4 3.0 %fusion.161 = (f32[16,128]{1,0:T(8,128)}, f32[16,128,128]{1,2,0:T(8,128)}) fusion(bf16[128,16,64]{0,2,1:T(8,128)(2,1)S(1)} %bitcast.270, bf16[128,16,64]{0,2,1:T(8,128)(2,1)} %bitcast.290, pred[128,128]{0,1:T(8,128)(4,1)} %get-tuple-element.72), kind=kOutput, calls=%fused_computation.271 | convolution fusion | flops 34338816 | bytes 1597440 | tf_op jit(solution)/shard_map/qhd,khd->hqk/dot_general | solution.py:27
  165.3 5.7 %collective-permute-done.7 = bf16[1,2,128,1024]{3,2,1,0:T(8,128)(2,1)} collective-permute-done((bf16[1,2,128,1024]{3,2,1,0:T(8,128)(2,1)}, bf16[1,2,128,1024]{3,2,1,0:T(8,128)(2,1)}, u32[]{:S(2)}, u32[]{:S(2)}) %collective-permute-start.7) | collective-permute-done | bytes 524320 | tf_op jit(solution)/shard_map/ppermute | solution.py:14
  171.1 1.8 fusion.151
  172.9 1.8 copy.101
  174.7 1.8 copy.102
  176.5 2.9 %fusion.160 = (f32[16,128]{1,0:T(8,128)}, f32[16,128,128]{1,2,0:T(8,128)}) fusion(bf16[128,16,64]{0,2,1:T(8,128)(2,1)S(1)} %bitcast.271, bf16[128,16,64]{0,2,1:T(8,128)(2,1)} %bitcast.286, pred[128,128]{0,1:T(8,128)(4,1)} %get-tuple-element.68), kind=kOutput, calls=%fused_computation.270 | convolution fusion | flops 34338816 | bytes 1597440 | tf_op jit(solution)/shard_map/qhd,khd->hqk/dot_general | solution.py:27
  179.3 4.6 %fusion.150 = (bf16[1,1,1024,1024]{3,2,1,0:T(8,128)(2,1)}, bf16[1,1,1024,1024]{3,2,1,0:T(8,128)(2,1)}) fusion(bf16[1,2,1024,1024]{3,2,1,0:T(8,128)(2,1)} %all-gather.2.cloned.1.call-done), kind=kLoop, calls=%fused_computation.260 | loop fusion | bytes 8388608 | tf_op jit(solution)/shard_map/slice | solution.py:74
  184.0 4.0 %copy.105 = bf16[1,1,1024,1024]{2,3,1,0:T(8,128)(2,1)} copy(bf16[1,1,1024,1024]{3,2,1,0:T(8,128)(2,1)} %get-tuple-element.45) | data formatting | bytes 4194304 | tf_op jit(solution)/shard_map/slice | solution.py:75
  187.9 4.0 %copy.104 = bf16[1,1,1024,1024]{2,3,1,0:T(8,128)(2,1)} copy(bf16[1,1,1024,1024]{3,2,1,0:T(8,128)(2,1)} %get-tuple-element.44) | data formatting | bytes 4194304 | tf_op jit(solution)/shard_map/slice | solution.py:74
  192.0 3.3 %fusion = (f32[16,128]{1,0:T(8,128)S(1)}, f32[16,128,1024]{2,1,0:T(8,128)S(1)}) fusion(pred[128,1024]{1,0:T(8,128)(4,1)S(1)} %iota_compare_fusion, bf16[128,16,64]{0,2,1:T(8,128)(2,1)S(1)} %bitcast.272, bf16[1024,16,64]{0,2,1:T(8,128)(2,1)} %bitcast.273), kind=kOutput, calls=%fused_computation.2 | convolution fusion | flops 274724864 | bytes 10887168 | tf_op jit(solution)/shard_map/qhd,khd->hqk/dot_general | solution.py:27
  195.4 2.5 %fusion.1 = f32[16,128]{1,0:T(8,128)S(1)} fusion(f32[16,128,1024]{2,1,0:T(8,128)S(1)} %get-tuple-element.77, f32[16,128]{1,0:T(8,128)S(1)} %get-tuple-element.35, pred[128,1024]{1,0:T(8,128)(4,1)S(1)} %iota_compare_fusion), kind=kLoop, calls=%fused_computation.3 | loop fusion | flops 10483712 | bytes 8536064 | tf_op jit(solution)/shard_map/reduce_sum | solution.py:32
  198.1 2.2 %fusion.15 = f32[128,16,64]{0,2,1:T(8,128)S(1)} fusion(bf16[1024,16,64]{0,2,1:T(8,128)(2,1)S(1)} %bitcast.274, f32[16,128,1024]{2,1,0:T(8,128)S(1)} %get-tuple-element.77, f32[16,128]{1,0:T(8,128)S(1)} %get-tuple-element.35, pred[128,1024]{1,0:T(8,128)(4,1)S(1)} %iota_compare_fusion), kind=kOutput, calls=%fused_computation.25 | convolution fusion | flops 278921216 | bytes 11149312 | tf_op jit(solution)/shard_map/hqk,khd->hqd/dot_general | solution.py:34
  204.9 0.3 fusion.38
  205.2 0.9 copy.106
  (134 shorter events, 5.0 us)
Async XLA Ops:
  6.5 172.8 %all-gather.2.cloned.1.call-start = ((), (), s32[]{:S(2)}) async-start(), calls=%async_computation | async-start | bytes 4259840 | tf_op jit(solution)/shard_map/all_gather | solution.py:70
  7.3 23.0 %collective-permute-start = (bf16[1,2,128,1024]{3,2,1,0:T(8,128)(2,1)}, bf16[1,2,128,1024]{3,2,1,0:T(8,128)(2,1)S(1)}, u32[]{:S(2)}, u32[]{:S(2)}) collective-permute-start(bf16[1,2,128,1024]{3,2,1,0:T(8,128)(2,1)} %param.5), channel_id=1, source_target_pairs={{0,1},{1,2},{2,3},{3,4},{4,5},{5,6},{6,7},{7,8},{8,9},{9,10},{10,1... | collective-permute-start | bytes 1572872 | tf_op jit(solution)/shard_map/ppermute | solution.py:14
  30.2 20.3 %collective-permute-start.1 = (bf16[1,2,128,1024]{3,2,1,0:T(8,128)(2,1)S(1)}, bf16[1,2,128,1024]{3,2,1,0:T(8,128)(2,1)S(1)}, u32[]{:S(2)}, u32[]{:S(2)}) collective-permute-start(bf16[1,2,128,1024]{3,2,1,0:T(8,128)(2,1)S(1)} %collective-permute-done), channel_id=1, source_target_pairs={{0,1},{1,2},{2,3},{3,4},{4,5},{5,6},{6,7},{7,8},{8,9},{9,10},{10,1... | collective-permute-start | bytes 1572872 | tf_op jit(solution)/shard_map/ppermute | solution.py:14
  33.3 59.5 %copy-start.21 = (pred[128,128]{0,1:T(8,128)(4,1)}, pred[128,128]{0,1:T(8,128)(4,1)S(1)}, u32[]{:S(2)}) copy-start(pred[128,128]{0,1:T(8,128)(4,1)S(1)} %get-tuple-element.69) | copy-start | bytes 49156
  33.3 59.5 %copy-start.23 = (pred[128,128]{0,1:T(8,128)(4,1)}, pred[128,128]{0,1:T(8,128)(4,1)S(1)}, u32[]{:S(2)}) copy-start(pred[128,128]{0,1:T(8,128)(4,1)S(1)} %get-tuple-element.67) | copy-start | bytes 49156
  50.5 21.7 %copy-start.15 = (bf16[1,2,128,1024]{3,2,1,0:T(8,128)(2,1)}, bf16[1,2,128,1024]{3,2,1,0:T(8,128)(2,1)S(1)}, u32[]{:S(2)}) copy-start(bf16[1,2,128,1024]{3,2,1,0:T(8,128)(2,1)S(1)} %collective-permute-done.1) | copy-start | bytes 1572868
  50.5 19.7 %collective-permute-start.2 = (bf16[1,2,128,1024]{3,2,1,0:T(8,128)(2,1)S(1)}, bf16[1,2,128,1024]{3,2,1,0:T(8,128)(2,1)}, u32[]{:S(2)}, u32[]{:S(2)}) collective-permute-start(bf16[1,2,128,1024]{3,2,1,0:T(8,128)(2,1)S(1)} %collective-permute-done.1), channel_id=1, source_target_pairs={{0,1},{1,2},{2,3},{3,4},{4,5},{5,6},{6,7},{7,8},{8,9},{9,10},{10,1... | collective-permute-start | bytes 1572872 | tf_op jit(solution)/shard_map/ppermute | solution.py:14
  70.2 20.6 %collective-permute-start.3 = (bf16[1,2,128,1024]{3,2,1,0:T(8,128)(2,1)}, bf16[1,2,128,1024]{3,2,1,0:T(8,128)(2,1)}, u32[]{:S(2)}, u32[]{:S(2)}) collective-permute-start(bf16[1,2,128,1024]{3,2,1,0:T(8,128)(2,1)} %collective-permute-done.2), channel_id=1, source_target_pairs={{0,1},{1,2},{2,3},{3,4},{4,5},{5,6},{6,7},{7,8},{8,9},{9,10},{10,1... | collective-permute-start | bytes 1572872 | tf_op jit(solution)/shard_map/ppermute | solution.py:14
  90.8 20.3 %collective-permute-start.4 = (bf16[1,2,128,1024]{3,2,1,0:T(8,128)(2,1)}, bf16[1,2,128,1024]{3,2,1,0:T(8,128)(2,1)}, u32[]{:S(2)}, u32[]{:S(2)}) collective-permute-start(bf16[1,2,128,1024]{3,2,1,0:T(8,128)(2,1)} %collective-permute-done.3), channel_id=1, source_target_pairs={{0,1},{1,2},{2,3},{3,4},{4,5},{5,6},{6,7},{7,8},{8,9},{9,10},{10,1... | collective-permute-start | bytes 1572872 | tf_op jit(solution)/shard_map/ppermute | solution.py:14
  111.1 20.7 %collective-permute-start.5 = (bf16[1,2,128,1024]{3,2,1,0:T(8,128)(2,1)}, bf16[1,2,128,1024]{3,2,1,0:T(8,128)(2,1)}, u32[]{:S(2)}, u32[]{:S(2)}) collective-permute-start(bf16[1,2,128,1024]{3,2,1,0:T(8,128)(2,1)} %collective-permute-done.4), channel_id=1, source_target_pairs={{0,1},{1,2},{2,3},{3,4},{4,5},{5,6},{6,7},{7,8},{8,9},{9,10},{10,1... | collective-permute-start | bytes 1572872 | tf_op jit(solution)/shard_map/ppermute | solution.py:14
  131.9 19.7 %collective-permute-start.6 = (bf16[1,2,128,1024]{3,2,1,0:T(8,128)(2,1)}, bf16[1,2,128,1024]{3,2,1,0:T(8,128)(2,1)}, u32[]{:S(2)}, u32[]{:S(2)}) collective-permute-start(bf16[1,2,128,1024]{3,2,1,0:T(8,128)(2,1)} %collective-permute-done.5), channel_id=1, source_target_pairs={{0,1},{1,2},{2,3},{3,4},{4,5},{5,6},{6,7},{7,8},{8,9},{9,10},{10,1... | collective-permute-start | bytes 1572872 | tf_op jit(solution)/shard_map/ppermute | solution.py:14
  144.4 9.3 %copy-start.33 = (f32[16,128]{1,0:T(8,128)}, f32[16,128]{1,0:T(8,128)S(1)}, u32[]{:S(2)}) copy-start(f32[16,128]{1,0:T(8,128)S(1)} %get-tuple-element.82) | copy-start | bytes 24580
  151.6 19.4 %collective-permute-start.7 = (bf16[1,2,128,1024]{3,2,1,0:T(8,128)(2,1)}, bf16[1,2,128,1024]{3,2,1,0:T(8,128)(2,1)}, u32[]{:S(2)}, u32[]{:S(2)}) collective-permute-start(bf16[1,2,128,1024]{3,2,1,0:T(8,128)(2,1)} %collective-permute-done.6), channel_id=1, source_target_pairs={{0,1},{1,2},{2,3},{3,4},{4,5},{5,6},{6,7},{7,8},{8,9},{9,10},{10,1... | collective-permute-start | bytes 1572872 | tf_op jit(solution)/shard_map/ppermute | solution.py:14
  191.9 3.4 %copy-start.27 = (f32[16,128]{1,0:T(8,128)S(1)}, f32[16,128]{1,0:T(8,128)}, u32[]{:S(2)}) copy-start(f32[16,128]{1,0:T(8,128)} %get-tuple-element.94) | copy-start | bytes 24580
  191.9 3.4 %copy-start.28 = (f32[16,128]{1,0:T(8,128)S(1)}, f32[16,128]{1,0:T(8,128)}, u32[]{:S(2)}) copy-start(f32[16,128]{1,0:T(8,128)} %get-tuple-element.92) | copy-start | bytes 24580
  191.9 3.4 %copy-start.29 = (f32[16,128]{1,0:T(8,128)S(1)}, f32[16,128]{1,0:T(8,128)}, u32[]{:S(2)}) copy-start(f32[16,128]{1,0:T(8,128)} %get-tuple-element.88) | copy-start | bytes 24580
  191.9 3.4 %copy-start.30 = (f32[16,128]{1,0:T(8,128)S(1)}, f32[16,128]{1,0:T(8,128)}, u32[]{:S(2)}) copy-start(f32[16,128]{1,0:T(8,128)} %get-tuple-element.84) | copy-start | bytes 24580
  191.9 3.5 %copy-start.31 = (f32[16,128]{1,0:T(8,128)S(1)}, f32[16,128]{1,0:T(8,128)}, u32[]{:S(2)}) copy-start(f32[16,128]{1,0:T(8,128)} %get-tuple-element.90) | copy-start | bytes 24580
  191.9 3.5 %copy-start.32 = (f32[16,128]{1,0:T(8,128)S(1)}, f32[16,128]{1,0:T(8,128)}, u32[]{:S(2)}) copy-start(f32[16,128]{1,0:T(8,128)} %get-tuple-element.86) | copy-start | bytes 24580
  191.9 3.5 %copy-start.34 = (f32[16,128]{1,0:T(8,128)S(1)}, f32[16,128]{1,0:T(8,128)}, u32[]{:S(2)}) copy-start(f32[16,128]{1,0:T(8,128)} %copy-done.33) | copy-start | bytes 24580
  191.9 3.5 %copy-start.35 = (f32[16,128]{1,0:T(8,128)S(1)}, f32[16,128]{1,0:T(8,128)}, u32[]{:S(2)}) copy-start(f32[16,128]{1,0:T(8,128)} %get-tuple-element.80) | copy-start | bytes 24580
  191.9 3.5 %copy-start.36 = (f32[16,128]{1,0:T(8,128)S(1)}, f32[16,128]{1,0:T(8,128)}, u32[]{:S(2)}) copy-start(f32[16,128]{1,0:T(8,128)} %get-tuple-element.78) | copy-start | bytes 24580
  191.9 6.0 %copy-start.6 = (bf16[1,1,1024,1024]{2,3,1,0:T(8,128)(2,1)S(1)}, bf16[1,1,1024,1024]{2,3,1,0:T(8,128)(2,1)}, u32[]{:S(2)}) copy-start(bf16[1,1,1024,1024]{2,3,1,0:T(8,128)(2,1)} %copy.105) | copy-start | bytes 6291460
  197.9 2.4 %copy-start.5 = (f32[16,128,128]{1,2,0:T(8,128)S(1)}, f32[16,128,128]{1,2,0:T(8,128)}, u32[]{:S(2)}) copy-start(f32[16,128,128]{1,2,0:T(8,128)} %get-tuple-element.79) | copy-start | bytes 3145732
  198.0 2.4 %copy-start.26 = (pred[128,128]{0,1:T(8,128)(4,1)S(1)}, pred[128,128]{0,1:T(8,128)(4,1)}, u32[]{:S(2)}) copy-start(pred[128,128]{0,1:T(8,128)(4,1)} %get-tuple-element.68) | copy-start | bytes 49156
  198.0 2.6 %copy-start.4 = (f32[16,128,128]{1,2,0:T(8,128)S(1)}, f32[16,128,128]{1,2,0:T(8,128)}, u32[]{:S(2)}) copy-start(f32[16,128,128]{1,2,0:T(8,128)} %get-tuple-element.81) | copy-start | bytes 3145732
  198.0 2.6 %copy-start.18 = (pred[128,128]{0,1:T(8,128)(4,1)S(1)}, pred[128,128]{0,1:T(8,128)(4,1)}, u32[]{:S(2)}) copy-start(pred[128,128]{0,1:T(8,128)(4,1)} %get-tuple-element.72) | copy-start | bytes 49156
  198.0 2.8 %copy-start.3 = (f32[16,128,128]{1,2,0:T(8,128)S(1)}, f32[16,128,128]{1,2,0:T(8,128)}, u32[]{:S(2)}) copy-start(f32[16,128,128]{1,2,0:T(8,128)} %get-tuple-element.83) | copy-start | bytes 3145732
  198.0 3.1 %copy-start.2 = (f32[16,128,128]{1,2,0:T(8,128)S(1)}, f32[16,128,128]{1,2,0:T(8,128)}, u32[]{:S(2)}) copy-start(f32[16,128,128]{1,2,0:T(8,128)} %get-tuple-element.85) | copy-start | bytes 3145732
  198.0 3.1 %copy-start.19 = (pred[128,128]{0,1:T(8,128)(4,1)S(1)}, pred[128,128]{0,1:T(8,128)(4,1)}, u32[]{:S(2)}) copy-start(pred[128,128]{0,1:T(8,128)(4,1)} %get-tuple-element.70) | copy-start | bytes 49156
  198.0 3.3 %copy-start.1 = (f32[16,128,128]{1,2,0:T(8,128)S(1)}, f32[16,128,128]{1,2,0:T(8,128)}, u32[]{:S(2)}) copy-start(f32[16,128,128]{1,2,0:T(8,128)} %get-tuple-element.87) | copy-start | bytes 3145732
  198.0 3.3 %copy-start.16 = (pred[128,128]{0,1:T(8,128)(4,1)S(1)}, pred[128,128]{0,1:T(8,128)(4,1)}, u32[]{:S(2)}) copy-start(pred[128,128]{0,1:T(8,128)(4,1)} %get-tuple-element.75) | copy-start | bytes 49156
  198.0 3.5 %copy-start = (f32[16,128,128]{1,2,0:T(8,128)S(1)}, f32[16,128,128]{1,2,0:T(8,128)}, u32[]{:S(2)}) copy-start(f32[16,128,128]{1,2,0:T(8,128)} %get-tuple-element.89) | copy-start | bytes 3145732
  198.0 3.5 %copy-start.17 = (pred[128,128]{0,1:T(8,128)(4,1)S(1)}, pred[128,128]{0,1:T(8,128)(4,1)}, u32[]{:S(2)}) copy-start(pred[128,128]{0,1:T(8,128)(4,1)} %get-tuple-element.73) | copy-start | bytes 49156
  198.1 3.7 %copy-start.20 = (pred[128,128]{0,1:T(8,128)(4,1)S(1)}, pred[128,128]{0,1:T(8,128)(4,1)}, u32[]{:S(2)}) copy-start(pred[128,128]{0,1:T(8,128)(4,1)} %get-tuple-element.71) | copy-start | bytes 49156
  198.1 3.9 %copy-start.22 = (pred[128,128]{0,1:T(8,128)(4,1)S(1)}, pred[128,128]{0,1:T(8,128)(4,1)}, u32[]{:S(2)}) copy-start(pred[128,128]{0,1:T(8,128)(4,1)} %copy-done.21) | copy-start | bytes 49156
  200.3 1.9 copy-start.24
  200.3 2.1 copy-start.8
  200.3 2.1 copy-start.37
  200.3 2.1 copy-start.38
  200.3 2.4 %copy-start.39 = (f32[128,16]{0,1:T(8,128)S(1)}, f32[128,16]{0,1:T(8,128)}, u32[]{:S(2)}) copy-start(f32[128,16]{0,1:T(8,128)} %get-tuple-element.32) | copy-start | bytes 24580
  200.3 2.4 %copy-start.40 = (f32[128,16]{0,1:T(8,128)S(1)}, f32[128,16]{0,1:T(8,128)}, u32[]{:S(2)}) copy-start(f32[128,16]{0,1:T(8,128)} %get-tuple-element.33) | copy-start | bytes 24580
  200.3 2.4 %copy-start.41 = (f32[128,16]{0,1:T(8,128)S(1)}, f32[128,16]{0,1:T(8,128)}, u32[]{:S(2)}) copy-start(f32[128,16]{0,1:T(8,128)} %get-tuple-element.34) | copy-start | bytes 24580
  200.4 2.5 %copy-start.7 = (bf16[1,1,128,1024]{2,3,1,0:T(8,128)(2,1)S(1)}, bf16[1,1,128,1024]{2,3,1,0:T(8,128)(2,1)}, u32[]{:S(2)}) copy-start(bf16[1,1,128,1024]{2,3,1,0:T(8,128)(2,1)} %copy.81) | copy-start | bytes 786436
  200.4 2.7 %copy-start.9 = (bf16[1,1,128,1024]{2,3,1,0:T(8,128)(2,1)S(1)}, bf16[1,1,128,1024]{2,3,1,0:T(8,128)(2,1)}, u32[]{:S(2)}) copy-start(bf16[1,1,128,1024]{2,3,1,0:T(8,128)(2,1)} %copy.84) | copy-start | bytes 786436
  200.4 3.0 %copy-start.10 = (bf16[1,1,128,1024]{2,3,1,0:T(8,128)(2,1)S(1)}, bf16[1,1,128,1024]{2,3,1,0:T(8,128)(2,1)}, u32[]{:S(2)}) copy-start(bf16[1,1,128,1024]{2,3,1,0:T(8,128)(2,1)} %copy.87) | copy-start | bytes 786436
  200.8 2.9 %copy-start.11 = (bf16[1,1,128,1024]{2,3,1,0:T(8,128)(2,1)S(1)}, bf16[1,1,128,1024]{2,3,1,0:T(8,128)(2,1)}, u32[]{:S(2)}) copy-start(bf16[1,1,128,1024]{2,3,1,0:T(8,128)(2,1)} %copy.90) | copy-start | bytes 786436
  201.3 2.7 %copy-start.12 = (bf16[1,1,128,1024]{2,3,1,0:T(8,128)(2,1)S(1)}, bf16[1,1,128,1024]{2,3,1,0:T(8,128)(2,1)}, u32[]{:S(2)}) copy-start(bf16[1,1,128,1024]{2,3,1,0:T(8,128)(2,1)} %copy.93) | copy-start | bytes 786436
  201.9 2.4 %copy-start.13 = (bf16[1,1,128,1024]{2,3,1,0:T(8,128)(2,1)S(1)}, bf16[1,1,128,1024]{2,3,1,0:T(8,128)(2,1)}, u32[]{:S(2)}) copy-start(bf16[1,1,128,1024]{2,3,1,0:T(8,128)(2,1)} %copy.96) | copy-start | bytes 786436
  202.4 2.2 %copy-start.14 = (bf16[1,1,128,1024]{2,3,1,0:T(8,128)(2,1)S(1)}, bf16[1,1,128,1024]{2,3,1,0:T(8,128)(2,1)}, u32[]{:S(2)}) copy-start(bf16[1,1,128,1024]{2,3,1,0:T(8,128)(2,1)} %copy.99) | copy-start | bytes 786436
  202.8 2.1 copy-start.25
Sparse Core Ops, SparseCore 0:
  10.7 129.4 all-gather.1
where the time goes:
time: 214 us; the launch traced here: 213 us
  waiting for transfers between devices  89.5 us (42%)
  local copies, waits for them, and re-layouts  55 us (26%)
  matrix products  28.8 us (13%)
  starting transfers between devices  15.5 us (7%)
  between operations  14.5 us (7%)
  other arithmetic  9.61 us (4%)
    ppermute x8, waiting for transfers between devices, from_behind(): return lax.ppermute(block, axis, route)  88.8 us
    slice x18, local copies, waits for them, and re-layouts, near_block(): vals = block[0, 1].reshape(tok_rows, HEADS, HEAD)  28.4 us
    dot_general x10, matrix products, absorb(): jnp.einsum('qhd,khd->hqk', query, keys, preferred_element_type=jnp.float32)  24 us
    ppermute x8, starting transfers between devices, from_behind(): return lax.ppermute(block, axis, route)  15.5 us
    slice x9, local copies, waits for them, and re-layouts, near_block(): keys = block[0, 0].reshape(tok_rows, HEADS, HEAD)  11.9 us
    slice x2, local copies, waits for them, and re-layouts, on_device(): keys = piece[0, 0].reshape(count, HEADS, HEAD)  8.58 us
    dot_general x10, matrix products, absorb(): jnp.einsum('hqk,khd->hqd', rounded, vals, preferred_element_type=jnp.floa...  4.77 us
    reduce_sum x10, other arithmetic, absorb(): new_total = running_total * factor + jnp.sum(weight, axis=-1)  4.29 us
  transfers between devices with their start and end apart: 9, of which 8 were waited for; matrix products, arithmetic and copies ran while one was open for 32% of the time, Pallas kernels for 0%

commit v1 on v0

v1 whole, which is shorter than its diff:
```python
import functools

import jax
import jax.numpy as jnp
from jax import lax
from jax.experimental import pallas as pl
from jax.experimental.pallas import tpu as pltpu
from jax.sharding import PartitionSpec as P

HEADS = 16
HEAD = 64
WIN = 1024
REQS = 12
ROW = 8
RING = 8
TOK = 128
PRE = 16
LANES = 128
MESH = pl.DeviceIdType.MESH


def place():
    grp = lax.axis_index("grp")
    me = lax.axis_index("req")
    return grp, me // ROW, me % ROW


def cols(number):
    return pl.ds(pl.multiple_of(number * LANES, LANES), LANES)


def rows(number, size, base=0):
    return pl.ds(pl.multiple_of(base + number * size, size), size)


def gather_kernel(q_ref, kv_ref, pre_ref, q_out, kv_out, pre_out,
                  q_own, kv_own, pre_own, a2a_send, a2a_recv, fwd_send, fwd_recv,
                  ring_send, ring_recv, local):
    grp, y, s = place()

    def peer(k):
        return (grp, y * ROW + (s + k) % ROW)

    up = (grp, ((y + 1) % RING) * ROW + s)
    down = (grp, ((y + RING - 1) % RING) * ROW + s)

    own_in = [
        pltpu.make_async_copy(pre_ref.at[0, :, :, cols(s)], pre_own, local.at[0]),
        pltpu.make_async_copy(kv_ref.at[0, :, :, cols(s)], kv_own, local.at[1]),
        pltpu.make_async_copy(q_ref.at[0, :, cols(s)], q_own, local.at[2]),
    ]
    for copy in own_in:
        copy.start()

    barrier = pltpu.get_barrier_semaphore()
    for k in range(1, ROW):
        pl.semaphore_signal(barrier, 1, device_id=peer(k), device_id_type=MESH)
    pl.semaphore_signal(barrier, 1, device_id=up, device_id_type=MESH)
    pl.semaphore_signal(barrier, 1, device_id=down, device_id_type=MESH)
    pl.semaphore_wait(barrier, ROW + 1)

    def send(src, dst, send_sem, recv_sem, to):
        copy = pltpu.make_async_remote_copy(
            src, dst, send_sem, recv_sem, device_id=to, device_id_type=MESH)
        copy.start()
        return copy

    order = (4, 2, 6, 3, 5, 1, 7)
    pre_sent = {}
    for k in order:
        t = (s + k) % ROW
        pre_sent[k] = send(pre_ref.at[0, :, :, cols(t)], pre_out.at[:, rows(y * ROW + s, PRE)],
                           a2a_send.at[0, k], a2a_recv.at[0, k], peer(k))
    kv_fwd = {0: send(kv_ref.at[0, :, :, cols(s)], kv_out.at[:, rows(s, TOK)],
                      fwd_send.at[0], fwd_recv.at[0], up)}
    kv_sent = {}
    for k in order:
        t = (s + k) % ROW
        kv_sent[k] = send(kv_ref.at[0, :, :, cols(t)], kv_out.at[:, rows(ROW + s, TOK)],
                          a2a_send.at[1, k], a2a_recv.at[1, k], peer(k))
    q_sent = {}
    for k in order:
        t = (s + k) % ROW
        q_sent[k] = send(q_ref.at[0, :, cols(t)], q_out.at[rows(s, TOK)],
                         a2a_send.at[2, k], a2a_recv.at[2, k], peer(k))
    own_out = [
        pltpu.make_async_copy(pre_own, pre_out.at[:, rows(y * ROW + s, PRE)], local.at[3]),
        pltpu.make_async_copy(kv_own, kv_out.at[:, rows(ROW + s, TOK)], local.at[4]),
        pltpu.make_async_copy(q_own, q_out.at[rows(s, TOK)], local.at[5]),
    ]
    for before, after in zip(own_in, own_out):
        before.wait()
        after.start()

    own_out[0].wait()
    for k in order:
        pre_sent[k].wait_recv()

    def ring_step(way, step):
        block = (y + RING - step) % RING if way == 0 else (y + step) % RING
        part = pre_out.at[:, rows(block, PRE * ROW)]
        return send(part, part, ring_send.at[way, step], ring_recv.at[way, step], up if way == 0 else down)

    steps = {(0, 0): ring_step(0, 0), (1, 0): ring_step(1, 0)}

    def forward(k):
        origin = (s + ROW - k) % ROW
        kv_sent[k].wait_recv()
        kv_fwd[k] = send(kv_out.at[:, rows(ROW + origin, TOK)], kv_out.at[:, rows(origin, TOK)],
                         fwd_send.at[k], fwd_recv.at[k], up)

    forward(4)
    forward(2)
    for step in range(1, 4):
        for way in range(2):
            if (way, step - 1) in steps and (way == 1 or step < 3):
                steps[way, step - 1].wait_recv()
                steps[way, step] = ring_step(way, step)
        if step == 1:
            forward(6)
            forward(3)
        if step == 2:
            forward(5)
            forward(1)
    forward(7)
    steps[0, 2].wait_recv()
    steps[1, 3].wait_recv()
    for k in order:
        q_sent[k].wait_recv()
    for k in range(ROW):
        kv_fwd[k].wait_recv()
    for copy in (*pre_sent.values(), *kv_sent.values(), *q_sent.values(), *kv_fwd.values(),
                 *steps.values()):
        copy.wait_send()
    own_out[1].wait()
    own_out[2].wait()


def attend_kernel(len_ref, q_ref, kv_ref, pre_ref, o_ref):
    block = pl.program_id(0)
    y = lax.axis_index("req") // ROW
    first = y * (ROW * TOK) + block * TOK
    token = first + lax.broadcasted_iota(jnp.int32, (TOK, 1), 0)
    start = jnp.zeros((TOK, 1), jnp.int32)
    end = jnp.int32(0)
    for r in range(REQS):
        end = end + len_ref[0, r]
        start = jnp.where(token >= end, end, start)
    lowest = jnp.maximum(start, token - (WIN - 1))
    offset = token - start
    lane = lax.broadcasted_iota(jnp.int32, (TOK, LANES), 1)
    q = q_ref[...]
    zero = jnp.zeros_like(q)
    both = jnp.concatenate([jnp.where(lane < HEAD, q, zero), jnp.where(lane >= HEAD, q, zero)], axis=0)
    span = WIN + TOK
    window = pl.ds(pl.multiple_of(block * TOK, TOK), span)
    contract = (((1,), (1,)), ((), ()))
    near = lax.dot_general(both, kv_ref[0, window, :], contract, preferred_element_type=jnp.float32)
    far = lax.dot_general(both, pre_ref[0], contract, preferred_element_type=jnp.float32)
    key = first - WIN + lax.broadcasted_iota(jnp.int32, (TOK, span), 1)
    near_mask = (key >= lowest) & (key <= token)
    far_mask = lax.broadcasted_iota(jnp.int32, (TOK, WIN), 1) > offset
    near = jnp.where(near_mask[None], near.reshape(2, TOK, span), -1e30)
    far = jnp.where(far_mask[None], far.reshape(2, TOK, WIN), -1e30)
    top = jnp.maximum(jnp.max(near, axis=-1, keepdims=True), jnp.max(far, axis=-1, keepdims=True))
    scale = 0.125 * 1.4426950408889634
    near = jnp.exp2((near - top) * scale)
    far = jnp.exp2((far - top) * scale)
    total = jnp.sum(near, axis=-1, keepdims=True) + jnp.sum(far, axis=-1, keepdims=True)
    added = jnp.dot(near.astype(jnp.bfloat16).reshape(2 * TOK, span), kv_ref[1, window, :],
                    preferred_element_type=jnp.float32)
    added += jnp.dot(far.astype(jnp.bfloat16).reshape(2 * TOK, WIN), pre_ref[1],
                     preferred_element_type=jnp.float32)
    added = added.reshape(2, TOK, LANES) / total
    o_ref[...] = jnp.where(lane < HEAD, added[0], added[1]).astype(jnp.bfloat16)


def return_kernel(o_ref, out_ref, own, send_sems, recv_sems, local):
    grp, y, s = place()
    own_in = pltpu.make_async_copy(o_ref.at[rows(s, TOK)], own, local.at[0])
    own_in.start()
    barrier = pltpu.get_barrier_semaphore()
    for k in range(1, ROW):
        pl.semaphore_signal(barrier, 1, device_id=(grp, y * ROW + (s + k) % ROW), device_id_type=MESH)
    pl.semaphore_wait(barrier, ROW - 1)
    copies = []
    for k in (4, 2, 6, 3, 5, 1, 7):
        t = (s + k) % ROW
        copy = pltpu.make_async_remote_copy(
            o_ref.at[rows(t, TOK)], out_ref.at[0, :, cols(s)], send_sems.at[k], recv_sems.at[k],
            device_id=(grp, y * ROW + t), device_id_type=MESH)
        copy.start()
        copies.append(copy)
    own_in.wait()
    own_out = pltpu.make_async_copy(own, out_ref.at[0, :, cols(s)], local.at[1])
    own_out.start()
    for copy in copies:
        copy.wait()
    own_out.wait()


def on_device(queries, suffix_kv, prefix_kv, lengths):
    bf16 = jnp.bfloat16
    anywhere = pl.BlockSpec(memory_space=pl.ANY)
    dma = pltpu.SemaphoreType.DMA
    q, kv, pre = pl.pallas_call(
        gather_kernel,
        out_shape=(
            jax.ShapeDtypeStruct((ROW * TOK, LANES), bf16),
            jax.ShapeDtypeStruct((2, 2 * ROW * TOK, LANES), bf16),
            jax.ShapeDtypeStruct((2, WIN, LANES), bf16),
        ),
        in_specs=[anywhere] * 3,
        out_specs=(anywhere,) * 3,
        scratch_shapes=[
            pltpu.VMEM((TOK, LANES), bf16),
            pltpu.VMEM((2, TOK, LANES), bf16),
            pltpu.VMEM((2, PRE, LANES), bf16),
            dma((3, ROW)), dma((3, ROW)), dma((ROW,)), dma((ROW,)),
            dma((2, 4)), dma((2, 4)), dma((6,)),
        ],
        compiler_params=pltpu.CompilerParams(collective_id=0, has_side_effects=True),
        name="gather",
    )(queries, suffix_kv, prefix_kv)
    mixed = pl.pallas_call(
        attend_kernel,
        grid=(ROW,),
        out_shape=jax.ShapeDtypeStruct((ROW * TOK, LANES), bf16),
        in_specs=[
            pl.BlockSpec(memory_space=pltpu.SMEM),
            pl.BlockSpec((TOK, LANES), lambda i: (i, 0)),
            pl.BlockSpec((2, 2 * ROW * TOK, LANES), lambda i: (0, 0, 0)),
            pl.BlockSpec((2, WIN, LANES), lambda i: (0, 0, 0)),
        ],
        out_specs=pl.BlockSpec((TOK, LANES), lambda i: (i, 0)),
        name="attend",
    )(lengths, q, kv, pre)
    return pl.pallas_call(
        return_kernel,
        out_shape=jax.ShapeDtypeStruct(queries.shape, bf16),
        in_specs=[anywhere],
        out_specs=anywhere,
        scratch_shapes=[pltpu.VMEM((TOK, LANES), bf16), dma((ROW,)), dma((ROW,)), dma((2,))],
        compiler_params=pltpu.CompilerParams(collective_id=1, has_side_effects=True),
        name="give_back",
    )(mixed)


def solution(mesh):
    in_specs = (
        P("grp", "req", None),
        P("grp", None, "req", None),
        P("grp", None, "req", None),
        P("grp", None),
    )
    return jax.shard_map(
        on_device, mesh=mesh, in_specs=in_specs, out_specs=P("grp", "req", None), check_vma=False
    )
```

time: 214 us -> 71.7 us (0.34)
  the two profiles are of different devices: /device:TPU:36 before, /device:TPU:67 now
where the time goes in v1:
time: 71.7 us; the launch traced here: 71.4 us
  Pallas kernels  69.8 us (97%)
  local copies, waits for them, and re-layouts  1.67 us (2%)
    pallas_call x1, Pallas kernels, on_device(): pl.pallas_call(gather_kernel, out_shape=(jax.ShapeDtypeStruct((ROW * TOK,...  43.3 us
    pallas_call x1, Pallas kernels, on_device(): pl.pallas_call(return_kernel, out_shape=jax.ShapeDtypeStruct(queries.shap...  14.2 us
    pallas_call x1, Pallas kernels, on_device(): pl.pallas_call(attend_kernel, grid=(ROW,), out_shape=jax.ShapeDtypeStruct...  12.2 us
    unnamed x1, local copies, waits for them, and re-layouts  1.67 us

profile of v1, /device:TPU:67, one launch (start us, length us, event | category | flops | bytes accessed | tf_op | source)
XLA Modules:
  0.0 71.4 jit_solution(16673227934811318486)
XLA Ops:
  0.0 43.3 %gather.1 = (bf16[1024,128]{1,0:T(8,128)(2,1)}, bf16[2,2048,128]{2,1,0:T(8,128)(2,1)}, bf16[2,1024,128]{2,1,0:T(8,128)(2,1)}) custom-call(bf16[1,128,1024]{2,1,0:T(8,128)(2,1)} %q_ref.1, bf16[1,2,128,1024]{3,2,1,0:T(8,128)(2,1)} %kv_ref.1, bf16[1,2,16,1024]{3,2,1,0:T(8,128)(2,1)} %pre_ref.1), custom_call_target="tpu_custom_call" | custom-call | tf_op jit(solution)/shard_map/gather/pallas_call | solution.py:206
  43.4 12.2 %attend.1.o_ref = bf16[1024,128]{1,0:T(8,128)(2,1)} custom-call(s32[1,12]{1,0:T(1,128)} %len_ref.1, bf16[1024,128]{1,0:T(8,128)(2,1)} %get-tuple-element.8.q_ref, bf16[2,2048,128]{2,1,0:T(8,128)(2,1)} %get-tuple-element.9.kv_ref, bf16[2,1024,128]{2,1,0:T(8,128)(2,1)} %get-tuple-element.10.pre_ref), custom_call_target="tpu_custom_call" | custom-call | tf_op jit(solution)/shard_map/attend/pallas_call | solution.py:225
  55.6 14.2 %give_back.1 = bf16[1,128,1024]{2,1,0:T(8,128)(2,1)} custom-call(bf16[1024,128]{1,0:T(8,128)(2,1)} %attend.1.o_ref), custom_call_target="tpu_custom_call" | custom-call | tf_op jit(solution)/shard_map/give_back/pallas_call | solution.py:238
  69.8 1.7 %copy.6 = bf16[1,128,1024]{2,1,0:T(8,128)(2,1)} copy(bf16[1,128,1024]{2,1,0:T(8,128)(2,1)} %give_back.1) | data formatting | bytes 524288

commit v2 on v0

v2 whole, which is shorter than its diff:
```python
import functools

import jax
import jax.numpy as jnp
from jax import lax
from jax.experimental import pallas as pl
from jax.experimental.pallas import tpu as pltpu
from jax.sharding import PartitionSpec as P

HEADS = 16
HEAD = 64
WIN = 1024
REQS = 12
ROW = 8
RING = 8
TOK = 128
PRE = 16
LANES = 128
MESH = pl.DeviceIdType.MESH


def place():
    grp = lax.axis_index("grp")
    me = lax.axis_index("req")
    return grp, me // ROW, me % ROW


def cols(number):
    return pl.ds(pl.multiple_of(number * LANES, LANES), LANES)


def rows(number, size, base=0):
    return pl.ds(pl.multiple_of(base + number * size, size), size)


ORDER = (4, 2, 6, 3, 5, 1, 7)
SPAN = WIN + TOK
CONTRACT = (((1,), (1,)), ((), ()))
SCALE = 0.125 * 1.4426950408889634


def whole_kernel(len_ref, q_ref, kv_ref, pre_ref, out_ref,
                 q_all, kv_all, pre_all, acc_all, top_all, sum_all, weight_all, mixed,
                 a2a_send, a2a_recv, fwd_send, fwd_recv, ring_send, ring_recv,
                 back_send, back_recv, local):
    grp, y, s = place()
    up = (grp, ((y + 1) % RING) * ROW + s)
    down = (grp, ((y + RING - 1) % RING) * ROW + s)

    def peer(k):
        return (grp, y * ROW + (s + k) % ROW)

    own = [
        pltpu.make_async_copy(pre_ref.at[0, :, :, cols(s)], pre_all.at[:, rows(y * ROW + s, PRE)], local.at[0]),
        pltpu.make_async_copy(q_ref.at[0, :, cols(s)], q_all.at[rows(s, TOK)], local.at[1]),
        pltpu.make_async_copy(kv_ref.at[0, :, :, cols(s)], kv_all.at[:, rows(ROW + s, TOK)], local.at[2]),
    ]
    for copy in own:
        copy.start()

    barrier = pltpu.get_barrier_semaphore()
    for k in range(1, ROW):
        pl.semaphore_signal(barrier, 1, device_id=peer(k), device_id_type=MESH)
    pl.semaphore_signal(barrier, 1, device_id=up, device_id_type=MESH)
    pl.semaphore_signal(barrier, 1, device_id=down, device_id_type=MESH)
    pl.semaphore_wait(barrier, ROW + 1)

    def send(src, dst, send_sem, recv_sem, to):
        copy = pltpu.make_async_remote_copy(
            src, dst, send_sem, recv_sem, device_id=to, device_id_type=MESH)
        copy.start()
        return copy

    sent = {}
    for k in ORDER:
        t = (s + k) % ROW
        sent[0, k] = send(pre_ref.at[0, :, :, cols(t)], pre_all.at[:, rows(y * ROW + s, PRE)],
                          a2a_send.at[0, k], a2a_recv.at[0, k], peer(k))
    for k in ORDER:
        t = (s + k) % ROW
        sent[1, k] = send(q_ref.at[0, :, cols(t)], q_all.at[rows(s, TOK)],
                          a2a_send.at[1, k], a2a_recv.at[1, k], peer(k))
    for part in range(2):
        for k in ORDER:
            t = (s + k) % ROW
            sent[2 + part, k] = send(
                kv_ref.at[0, part, :, cols(t)], kv_all.at[part, rows(ROW + s, TOK)],
                a2a_send.at[2 + part, k], a2a_recv.at[2 + part, k], peer(k))

    own[0].wait()
    for k in ORDER:
        sent[0, k].wait_recv()
    steps = {}

    def ring_step(way, step):
        block = (y + RING - step) % RING if way == 0 else (y + step) % RING
        part = pre_all.at[:, rows(block, PRE * ROW)]
        steps[way, step] = send(part, part, ring_send.at[way, step], ring_recv.at[way, step],
                                up if way == 0 else down)

    ring_step(0, 0)
    ring_step(1, 0)
    forwarded = {}
    for part in range(2):
        forwarded[part, 0] = send(
            kv_ref.at[0, part, :, cols(s)], kv_all.at[part, rows(s, TOK)],
            fwd_send.at[part, 0], fwd_recv.at[part, 0], up)
    for step in range(1, 4):
        for way in range(2):
            steps[way, step - 1].wait_recv() if (way, step - 1) in steps else None
            if way == 1 or step < 3:
                ring_step(way, step)

    def forward(part, k):
        origin = (s + ROW - k) % ROW
        sent[2 + part, k].wait_recv()
        forwarded[part, k] = send(
            kv_all.at[part, rows(ROW + origin, TOK)], kv_all.at[part, rows(origin, TOK)],
            fwd_send.at[part, k], fwd_recv.at[part, k], up)

    steps[1, 3].wait_recv()
    own[1].wait()
    for k in ORDER:
        sent[1, k].wait_recv()

    def bounds(block):
        first = y * (ROW * TOK) + block * TOK
        token = first + lax.broadcasted_iota(jnp.int32, (TOK, 1), 0)
        start = jnp.zeros((TOK, 1), jnp.int32)
        end = jnp.int32(0)
        for r in range(REQS):
            end = end + len_ref[0, r]
            start = jnp.where(token >= end, end, start)
        return first, token, start

    lane = lax.broadcasted_iota(jnp.int32, (TOK, LANES), 1)

    def two_heads(block):
        q = q_all[rows(block, TOK), :]
        zero = jnp.zeros_like(q)
        return jnp.concatenate(
            [jnp.where(lane < HEAD, q, zero), jnp.where(lane >= HEAD, q, zero)], axis=0)

    def far_block(block, carry):
        first, token, start = bounds(block)
        score = lax.dot_general(two_heads(block), pre_all[0], CONTRACT, preferred_element_type=jnp.float32)
        mask = lax.broadcasted_iota(jnp.int32, (TOK, WIN), 1) > token - start
        score = jnp.where(mask[None], score.reshape(2, TOK, WIN), -1e30).reshape(2 * TOK, WIN)
        top = jnp.max(score, axis=-1, keepdims=True)
        weight = jnp.exp2((score - top) * SCALE)
        here = rows(block, 2 * TOK)
        top_all[here, :] = top
        sum_all[here, :] = jnp.sum(weight, axis=-1, keepdims=True)
        acc_all[here, :] = jnp.dot(weight.astype(jnp.bfloat16), pre_all[1], preferred_element_type=jnp.float32)
        return carry

    def near_block(block, carry):
        first, token, start = bounds(block)
        window = pl.ds(pl.multiple_of(block * TOK, TOK), SPAN)
        score = lax.dot_general(
            two_heads(block), kv_all[0, window, :], CONTRACT, preferred_element_type=jnp.float32)
        key = first - WIN + lax.broadcasted_iota(jnp.int32, (TOK, SPAN), 1)
        mask = (key >= jnp.maximum(start, token - (WIN - 1))) & (key <= token)
        score = jnp.where(mask[None], score.reshape(2, TOK, SPAN), -1e30).reshape(2 * TOK, SPAN)
        here = rows(block, 2 * TOK)
        old = top_all[here, :]
        top = jnp.maximum(old, jnp.max(score, axis=-1, keepdims=True))
        factor = jnp.exp2((old - top) * SCALE)
        weight = jnp.exp2((score - top) * SCALE)
        total = sum_all[here, :] * factor + jnp.sum(weight, axis=-1, keepdims=True)
        weight_all[here, :] = weight.astype(jnp.bfloat16)
        sum_all[here, :] = total
        acc_all[here, :] = acc_all[here, :] * factor
        return carry

    def value_block(block):
        window = pl.ds(pl.multiple_of(block * TOK, TOK), SPAN)
        here = rows(block, 2 * TOK)
        added = acc_all[here, :] + jnp.dot(
            weight_all[here, :], kv_all[1, window, :], preferred_element_type=jnp.float32)
        added = (added / sum_all[here, :]).reshape(2, TOK, LANES)
        mixed[rows(block, TOK), :] = jnp.where(lane < HEAD, added[0], added[1]).astype(jnp.bfloat16)

    for part, blocks in ((0, far_block), (1, near_block)):
        for quarter in range(4):
            lax.fori_loop(2 * quarter, 2 * quarter + 2, blocks, 0)
            for k in ORDER[2 * quarter:2 * quarter + 2]:
                forward(part, k)
        if part == 0:
            own[2].wait()
        for k in range(ROW):
            forwarded[part, k].wait_recv()

    def back(k):
        t = (s + k) % ROW
        return pltpu.make_async_remote_copy(
            mixed.at[rows(t, TOK)], out_ref.at[0, :, cols(s)], back_send.at[k], back_recv.at[k],
            device_id=peer(k), device_id_type=MESH)

    def give_back(k, carry):
        value_block((s + k) % ROW)

        @pl.when(k > 1)
        def _():
            back(k - 1).start()

        return carry

    lax.fori_loop(1, ROW, give_back, 0)
    value_block(s)
    back(ROW - 1).start()
    mine = pltpu.make_async_copy(mixed.at[rows(s, TOK)], out_ref.at[0, :, cols(s)], local.at[3])
    mine.start()
    for copy in (*sent.values(), *forwarded.values(), *steps.values()):
        copy.wait_send()
    for k in range(1, ROW):
        back(k).wait()
    mine.wait()


def on_device(queries, suffix_kv, prefix_kv, lengths):
    bf16 = jnp.bfloat16
    anywhere = pl.BlockSpec(memory_space=pl.ANY)
    dma = pltpu.SemaphoreType.DMA
    tokens = ROW * TOK
    return pl.pallas_call(
        whole_kernel,
        out_shape=jax.ShapeDtypeStruct(queries.shape, bf16),
        in_specs=[pl.BlockSpec(memory_space=pltpu.SMEM)] + [anywhere] * 3,
        out_specs=anywhere,
        scratch_shapes=[
            pltpu.VMEM((tokens, LANES), bf16),
            pltpu.VMEM((2, 2 * tokens, LANES), bf16),
            pltpu.VMEM((2, WIN, LANES), bf16),
            pltpu.VMEM((2 * tokens, LANES), jnp.float32),
            pltpu.VMEM((2 * tokens, 1), jnp.float32),
            pltpu.VMEM((2 * tokens, 1), jnp.float32),
            pltpu.VMEM((2 * tokens, SPAN), bf16),
            pltpu.VMEM((tokens, LANES), bf16),
            dma((4, ROW)), dma((4, ROW)), dma((2, ROW)), dma((2, ROW)),
            dma((2, 4)), dma((2, 4)), dma((ROW,)), dma((ROW,)), dma((4,)),
        ],
        compiler_params=pltpu.CompilerParams(collective_id=0, has_side_effects=True),
        name="suffix_attention",
    )(lengths, queries, suffix_kv, prefix_kv)


def solution(mesh):
    in_specs = (
        P("grp", "req", None),
        P("grp", None, "req", None),
        P("grp", None, "req", None),
        P("grp", None),
    )
    return jax.shard_map(
        on_device, mesh=mesh, in_specs=in_specs, out_specs=P("grp", "req", None), check_vma=False
    )
```

time: 214 us -> 73.3 us (0.34)
  the two profiles are of different devices: /device:TPU:36 before, /device:TPU:71 now
where the time goes in v2:
time: 73.3 us; the launch traced here: 73.1 us
  Pallas kernels  71.4 us (97%)
  local copies, waits for them, and re-layouts  1.67 us (2%)
    pallas_call x1, Pallas kernels, on_device(): pl.pallas_call(whole_kernel, out_shape=jax.ShapeDtypeStruct(queries.shape...  71.4 us
    unnamed x1, local copies, waits for them, and re-layouts  1.67 us

profile of v2, /device:TPU:71, one launch (start us, length us, event | category | flops | bytes accessed | tf_op | source)
XLA Modules:
  0.0 73.1 jit_solution(16235914973838317203)
XLA Ops:
  0.0 71.4 %suffix_attention.1 = bf16[1,128,1024]{2,1,0:T(8,128)(2,1)} custom-call(s32[1,12]{1,0:T(1,128)} %len_ref.1, bf16[1,128,1024]{2,1,0:T(8,128)(2,1)} %q_ref.1, bf16[1,2,128,1024]{3,2,1,0:T(8,128)(2,1)} %kv_ref.1, bf16[1,2,16,1024]{3,2,1,0:T(8,128)(2,1)} %pre_ref.1), custom_call_target="tpu_custom_call" | custom-call | tf_op jit(solution)/shard_map/suffix_attention/pallas_call | solution.py:226
  71.4 1.7 %copy.6 = bf16[1,128,1024]{2,1,0:T(8,128)(2,1)} copy(bf16[1,128,1024]{2,1,0:T(8,128)(2,1)} %suffix_attention.1) | data formatting | bytes 524288

commit v3 on v2

--- a/solution.py
+++ b/solution.py
@@ -92,36 +92,47 @@
         sent[0, k].wait_recv()
     steps = {}
 
-    def ring_step(way, step):
+    def ring_step(way, step, half):
         block = (y + RING - step) % RING if way == 0 else (y + step) % RING
-        part = pre_all.at[:, rows(block, PRE * ROW)]
-        steps[way, step] = send(part, part, ring_send.at[way, step], ring_recv.at[way, step],
-                                up if way == 0 else down)
-
-    ring_step(0, 0)
-    ring_step(1, 0)
+        part = pre_all.at[half, rows(block, PRE * ROW)]
+        steps[way, step, half] = send(
+            part, part, ring_send.at[way, step, half], ring_recv.at[way, step, half],
+            up if way == 0 else down)
+
+    def ring_round(step):
+        for half in range(2):
+            for way in range(2):
+                if step and (way == 1 or step < 4):
+                    steps[way, step - 1, half].wait_recv()
+                if step < 3 + way:
+                    ring_step(way, step, half)
+
     forwarded = {}
-    for part in range(2):
-        forwarded[part, 0] = send(
-            kv_ref.at[0, part, :, cols(s)], kv_all.at[part, rows(s, TOK)],
-            fwd_send.at[part, 0], fwd_recv.at[part, 0], up)
-    for step in range(1, 4):
-        for way in range(2):
-            steps[way, step - 1].wait_recv() if (way, step - 1) in steps else None
-            if way == 1 or step < 3:
-                ring_step(way, step)
 
     def forward(part, k):
-        origin = (s + ROW - k) % ROW
-        sent[2 + part, k].wait_recv()
+        if k == 0:
+            source = kv_ref.at[0, part, :, cols(s)]
+        else:
+            sent[2 + part, k].wait_recv()
+            source = kv_all.at[part, rows(ROW + (s + ROW - k) % ROW, TOK)]
         forwarded[part, k] = send(
-            kv_all.at[part, rows(ROW + origin, TOK)], kv_all.at[part, rows(origin, TOK)],
+            source, kv_all.at[part, rows((s + ROW - k) % ROW, TOK)],
             fwd_send.at[part, k], fwd_recv.at[part, k], up)
 
-    steps[1, 3].wait_recv()
+    ring_round(0)
+    forward(0, 0)
+    ring_round(1)
+    forward(1, 0)
+    ring_round(2)
+    for k in ORDER[:3]:
+        forward(0, k)
+    ring_round(3)
+    for k in ORDER[3:]:
+        forward(0, k)
     own[1].wait()
     for k in ORDER:
         sent[1, k].wait_recv()
+    ring_round(4)
 
     def bounds(block):
         first = y * (ROW * TOK) + block * TOK
@@ -181,15 +192,13 @@
         added = (added / sum_all[here, :]).reshape(2, TOK, LANES)
         mixed[rows(block, TOK), :] = jnp.where(lane < HEAD, added[0], added[1]).astype(jnp.bfloat16)
 
-    for part, blocks in ((0, far_block), (1, near_block)):
-        for quarter in range(4):
-            lax.fori_loop(2 * quarter, 2 * quarter + 2, blocks, 0)
-            for k in ORDER[2 * quarter:2 * quarter + 2]:
-                forward(part, k)
-        if part == 0:
-            own[2].wait()
-        for k in range(ROW):
-            forwarded[part, k].wait_recv()
+    for quarter in range(4):
+        lax.fori_loop(2 * quarter, 2 * quarter + 2, far_block, 0)
+        for k in ORDER[2 * quarter:2 * quarter + 2]:
+            forward(1, k)
+    own[2].wait()
+    for k in range(ROW):
+        forwarded[0, k].wait_recv()
 
     def back(k):
         t = (s + k) % ROW
@@ -197,16 +206,29 @@
             mixed.at[rows(t, TOK)], out_ref.at[0, :, cols(s)], back_send.at[k], back_recv.at[k],
             device_id=peer(k), device_id_type=MESH)
 
-    def give_back(k, carry):
+    def near_first(k, carry):
+        return near_block((s + k) % ROW, carry)
+
+    def near_and_back(k, carry):
         value_block((s + k) % ROW)
-
-        @pl.when(k > 1)
+        near_block((s + k + 4) % ROW, carry)
+        back(k).start()
+        return carry
+
+    def late_back(k, carry):
+        value_block((s + k) % ROW)
+
+        @pl.when(k > 5)
         def _():
             back(k - 1).start()
 
         return carry
 
-    lax.fori_loop(1, ROW, give_back, 0)
+    lax.fori_loop(1, 5, near_first, 0)
+    for k in range(ROW):
+        forwarded[1, k].wait_recv()
+    lax.fori_loop(1, 5, near_and_back, 0)
+    lax.fori_loop(5, ROW, late_back, 0)
     value_block(s)
     back(ROW - 1).start()
     mine = pltpu.make_async_copy(mixed.at[rows(s, TOK)], out_ref.at[0, :, cols(s)], local.at[3])
@@ -238,7 +260,7 @@
             pltpu.VMEM((2 * tokens, SPAN), bf16),
             pltpu.VMEM((tokens, LANES), bf16),
             dma((4, ROW)), dma((4, ROW)), dma((2, ROW)), dma((2, ROW)),
-            dma((2, 4)), dma((2, 4)), dma((ROW,)), dma((ROW,)), dma((4,)),
+            dma((2, 4, 2)), dma((2, 4, 2)), dma((ROW,)), dma((ROW,)), dma((4,)),
         ],
         compiler_params=pltpu.CompilerParams(collective_id=0, has_side_effects=True),
         name="suffix_attention",

time: 73.3 us -> 65 us (0.89)
  the two profiles are of different devices: /device:TPU:71 before, /device:TPU:67 now
where the time goes in v3:
time: 65 us; the launch traced here: 64.8 us
  Pallas kernels  63.1 us (97%)
  local copies, waits for them, and re-layouts  1.67 us (3%)
    pallas_call x1, Pallas kernels, on_device(): pl.pallas_call(whole_kernel, out_shape=jax.ShapeDtypeStruct(queries.shape...  63.1 us
    unnamed x1, local copies, waits for them, and re-layouts  1.67 us

profile of v3, /device:TPU:67, one launch (start us, length us, event | category | flops | bytes accessed | tf_op | source)
XLA Modules:
  0.0 64.8 jit_solution(4954571942137594430)
XLA Ops:
  0.0 63.1 %suffix_attention.1 = bf16[1,128,1024]{2,1,0:T(8,128)(2,1)} custom-call(s32[1,12]{1,0:T(1,128)} %len_ref.1, bf16[1,128,1024]{2,1,0:T(8,128)(2,1)} %q_ref.1, bf16[1,2,128,1024]{3,2,1,0:T(8,128)(2,1)} %kv_ref.1, bf16[1,2,16,1024]{3,2,1,0:T(8,128)(2,1)} %pre_ref.1), custom_call_target="tpu_custom_call" | custom-call | tf_op jit(solution)/shard_map/suffix_attention/pallas_call | solution.py:248
  63.1 1.7 %copy.6 = bf16[1,128,1024]{2,1,0:T(8,128)(2,1)} copy(bf16[1,128,1024]{2,1,0:T(8,128)(2,1)} %suffix_attention.1) | data formatting | bytes 524288

commit v4 on v3

--- a/solution.py
+++ b/solution.py
@@ -80,13 +80,6 @@
         t = (s + k) % ROW
         sent[1, k] = send(q_ref.at[0, :, cols(t)], q_all.at[rows(s, TOK)],
                           a2a_send.at[1, k], a2a_recv.at[1, k], peer(k))
-    for part in range(2):
-        for k in ORDER:
-            t = (s + k) % ROW
-            sent[2 + part, k] = send(
-                kv_ref.at[0, part, :, cols(t)], kv_all.at[part, rows(ROW + s, TOK)],
-                a2a_send.at[2 + part, k], a2a_recv.at[2 + part, k], peer(k))
-
     own[0].wait()
     for k in ORDER:
         sent[0, k].wait_recv()
@@ -119,6 +112,13 @@
             source, kv_all.at[part, rows((s + ROW - k) % ROW, TOK)],
             fwd_send.at[part, k], fwd_recv.at[part, k], up)
 
+    for part in range(1):
+        for k in ORDER:
+            t = (s + k) % ROW
+            sent[2 + part, k] = send(
+                kv_ref.at[0, part, :, cols(t)], kv_all.at[part, rows(ROW + s, TOK)],
+                a2a_send.at[2 + part, k], a2a_recv.at[2 + part, k], peer(k))
+
     ring_round(0)
     forward(0, 0)
     ring_round(1)
@@ -126,6 +126,13 @@
     ring_round(2)
     for k in ORDER[:3]:
         forward(0, k)
+    for part in range(1, 2):
+        for k in ORDER:
+            t = (s + k) % ROW
+            sent[2 + part, k] = send(
+                kv_ref.at[0, part, :, cols(t)], kv_all.at[part, rows(ROW + s, TOK)],
+                a2a_send.at[2 + part, k], a2a_recv.at[2 + part, k], peer(k))
+
     ring_round(3)
     for k in ORDER[3:]:
         forward(0, k)

time: 65 us -> 56.9 us (0.88)
  the two profiles are of different devices: /device:TPU:67 before, /device:TPU:71 now
where the time goes in v4:
time: 56.9 us; the launch traced here: 56.7 us
  Pallas kernels  55.1 us (97%)
  local copies, waits for them, and re-layouts  1.67 us (3%)
    pallas_call x1, Pallas kernels, on_device(): pl.pallas_call(whole_kernel, out_shape=jax.ShapeDtypeStruct(queries.shape...  55.1 us
    unnamed x1, local copies, waits for them, and re-layouts  1.67 us

profile of v4, /device:TPU:71, one launch (start us, length us, event | category | flops | bytes accessed | tf_op | source)
XLA Modules:
  0.0 56.7 jit_solution(17880521257222715605)
XLA Ops:
  0.0 55.1 %suffix_attention.1 = bf16[1,128,1024]{2,1,0:T(8,128)(2,1)} custom-call(s32[1,12]{1,0:T(1,128)} %len_ref.1, bf16[1,128,1024]{2,1,0:T(8,128)(2,1)} %q_ref.1, bf16[1,2,128,1024]{3,2,1,0:T(8,128)(2,1)} %kv_ref.1, bf16[1,2,16,1024]{3,2,1,0:T(8,128)(2,1)} %pre_ref.1), custom_call_target="tpu_custom_call" | custom-call | tf_op jit(solution)/shard_map/suffix_attention/pallas_call | solution.py:255
  55.1 1.7 %copy.6 = bf16[1,128,1024]{2,1,0:T(8,128)(2,1)} copy(bf16[1,128,1024]{2,1,0:T(8,128)(2,1)} %suffix_attention.1) | data formatting | bytes 524288

commit v5 on v4

--- a/solution.py
+++ b/solution.py
@@ -33,7 +33,7 @@
     return pl.ds(pl.multiple_of(base + number * size, size), size)
 
 
-ORDER = (4, 2, 6, 3, 5, 1, 7)
+ORDER = (2, 6, 4, 1, 7, 3, 5)
 SPAN = WIN + TOK
 CONTRACT = (((1,), (1,)), ((), ()))
 SCALE = 0.125 * 1.4426950408889634
@@ -218,24 +218,15 @@
 
     def near_and_back(k, carry):
         value_block((s + k) % ROW)
-        near_block((s + k + 4) % ROW, carry)
+        near_block((s + k + 2) % ROW, carry)
         back(k).start()
         return carry
 
-    def late_back(k, carry):
-        value_block((s + k) % ROW)
-
-        @pl.when(k > 5)
-        def _():
-            back(k - 1).start()
-
-        return carry
-
-    lax.fori_loop(1, 5, near_first, 0)
+    lax.fori_loop(1, 3, near_first, 0)
     for k in range(ROW):
         forwarded[1, k].wait_recv()
-    lax.fori_loop(1, 5, near_and_back, 0)
-    lax.fori_loop(5, ROW, late_back, 0)
+    lax.fori_loop(1, 7, near_and_back, 0)
+    value_block((s + ROW - 1) % ROW)
     value_block(s)
     back(ROW - 1).start()
     mine = pltpu.make_async_copy(mixed.at[rows(s, TOK)], out_ref.at[0, :, cols(s)], local.at[3])

time: 56.9 us -> 57.2 us (level)
  no operation moved by 1% of the time
where the time goes in v5:
time: 57.2 us; the launch traced here: 57 us
  Pallas kernels  55.3 us (97%)
  local copies, waits for them, and re-layouts  1.67 us (3%)
    pallas_call x1, Pallas kernels, on_device(): pl.pallas_call(whole_kernel, out_shape=jax.ShapeDtypeStruct(queries.shape...  55.3 us
    unnamed x1, local copies, waits for them, and re-layouts  1.67 us

profile of v5, /device:TPU:71, one launch (start us, length us, event | category | flops | bytes accessed | tf_op | source)
XLA Modules:
  0.0 57.0 jit_solution(4261954708867991614)
XLA Ops:
  0.0 55.3 %suffix_attention.1 = bf16[1,128,1024]{2,1,0:T(8,128)(2,1)} custom-call(s32[1,12]{1,0:T(1,128)} %len_ref.1, bf16[1,128,1024]{2,1,0:T(8,128)(2,1)} %q_ref.1, bf16[1,2,128,1024]{3,2,1,0:T(8,128)(2,1)} %kv_ref.1, bf16[1,2,16,1024]{3,2,1,0:T(8,128)(2,1)} %pre_ref.1), custom_call_target="tpu_custom_call" | custom-call | tf_op jit(solution)/shard_map/suffix_attention/pallas_call | solution.py:246
  55.3 1.7 %copy.6 = bf16[1,128,1024]{2,1,0:T(8,128)(2,1)} copy(bf16[1,128,1024]{2,1,0:T(8,128)(2,1)} %suffix_attention.1) | data formatting | bytes 524288
